TPU v7x, 256 devices: a whole 4x4x8 slice. The times are simulated.
256 devices in a mesh: layer: 8 (over z_lo, core), feat: 32 (over x, y, z_hi).
Axes of the slice: x: 4, y: 4, z: 8 (z_hi: 2, z_lo: 4; z = z_hi * 4 + z_lo), core: 2. Of those that a mesh axis runs over, the one named last changes fastest.
Arguments:
- source: bfloat16 [512, 2304], P('feat', 'layer'), may hold values from -6 to 6
- enc_weight: bfloat16 [2304, 32768], P('layer', 'feat'), may hold values from -0.125 to 0.125
- enc_bias: float32 [32768], P('feat'), may hold values from -3 to 3
- dec_weight: bfloat16 [8, 32768, 2304], P('layer', 'feat'), may hold values from -0.03125 to 0.03125
- dec_bias: float32 [8, 2304], P('layer'), may hold values from -3 to 3
- targets: bfloat16 [8, 512, 2304], P('layer', 'feat'), may hold values from -6 to 6
Outputs:
- enc_grad: bfloat16 [2304, 32768], P('layer', 'feat')
- dec_grad: bfloat16 [8, 32768, 2304], P('layer', 'feat')
All inputs are finite; a program needn't handle non-finite values.
Results may differ from a plain program's by a relative error of at most 0.014.
Values may be sent and summed in bfloat16 or wider, within the bound.
A program may use at most 64 MiB of HBM per device.

v0:
```python
import jax
import jax.numpy as jnp
from jax import lax
from jax.sharding import PartitionSpec as P


def body(source, enc_weight, enc_bias, dec_weight, dec_bias, targets):
    source_rows = lax.all_gather(source, "feat", axis=0, tiled=True)
    partial_input = jnp.dot(source_rows, enc_weight, preferred_element_type=jnp.float32)
    preact = lax.psum(partial_input, "layer")
    preact = preact + enc_bias[None, :]
    active = jnp.maximum(preact, 0.0)
    features = (active * active).astype(jnp.bfloat16)
    decoder = dec_weight[0]
    picked = features
    rebuilt = lax.psum_scatter(
        jnp.dot(picked, decoder, preferred_element_type=jnp.float32).astype(jnp.bfloat16),
        "feat",
        scatter_dimension=0,
        tiled=True,
    ).astype(jnp.float32)
    rebuilt = rebuilt + dec_bias[0][None, :]
    residual = (rebuilt - targets[0].astype(jnp.float32)).astype(jnp.bfloat16)
    piece = lax.all_gather(residual, "feat", axis=0, tiled=True)
    picked = features
    weight_total = lax.dot_general(
        picked, piece, (((0,), (0,)), ((), ())), preferred_element_type=jnp.float32
    )
    grad_block = lax.dot_general(
        piece, decoder, (((1,), (1,)), ((), ())), preferred_element_type=jnp.float32
    )
    grad_total = grad_block
    weight_total, grad_total = (weight_total, grad_total)
    summed = lax.psum(grad_total, "layer")
    feat_grad = (2.0 * active * summed).astype(jnp.bfloat16)
    enc_grad = lax.dot_general(
        source_rows, feat_grad, (((0,), (0,)), ((), ())), preferred_element_type=jnp.float32
    ).astype(jnp.bfloat16)
    return (enc_grad, weight_total.astype(jnp.bfloat16)[None])


def solution(mesh):
    placed = (
        P("feat", "layer"),
        P("layer", "feat"),
        P("feat"),
        P("layer", "feat", None),
        P("layer", None),
        P("layer", "feat", None),
    )
    return jax.shard_map(
        body,
        mesh=mesh,
        in_specs=placed,
        out_specs=(P("layer", "feat"), P("layer", "feat", None)),
        check_vma=False,
    )
```

profile of v0, /device:TPU:1, one launch (start us, length us, event | category | flops | bytes accessed | tf_op | source)
XLA Modules:
  0.0 653.7 jit_solution(1544659206685551485)
XLA Ops:
  7.2 0.0 copy-start
  7.2 0.0 all-reduce.3.cloned.1.call-start
  7.2 108.7 %all_gather.6 = bf16[512,288]{1,0:T(8,128)(2,1)S(1)} all-gather(bf16[16,288]{1,0:T(8,128)(2,1)} %param.6), channel_id=1, replica_groups=mesh['layer'=8,'feat'=32] {'feat'}, dimensions={0}, use_global_device_ids=true | all-gather | bytes 304128 | tf_op jit(solution)/shard_map/all_gather | solution.py:8
  115.9 0.0 copy-done
  115.9 2.0 fusion.17
  117.9 0.0 all-reduce.3.cloned.1.call-update
  118.0 0.0 reduce-scatter.2.cloned.1.call-start
  118.0 85.1 %all-reduce.3.cloned.1.call-done = f32[512,1024]{1,0:T(8,128)} async-done(((f32[512,1024]{1,0:T(8,128)}), f32[512,1024]{1,0:T(8,128)}) %all-reduce.3.cloned.1.call-update) | async-done | bytes 2097168 | tf_op jit(solution)/shard_map/psum | solution.py:10
  203.1 0.0 copy-done.4
  203.1 7.0 %fusion.5 = bf16[512,2304]{1,0:T(8,128)(2,1)} fusion(bf16[1,1024,2304]{2,1,0:T(8,128)(2,1)} %param.9, f32[512,1024]{1,0:T(8,128)} %all-reduce.3.cloned.1.call-done, f32[1024]{0:T(1024)S(1)} %copy-done.4), kind=kOutput, calls=%fused_computation.6 | convolution fusion | flops 2419195904 | bytes 9179136 | tf_op jit(solution)/shard_map/dot_general | solution.py:17
  210.1 0.0 reduce-scatter.2.cloned.1.call-update
  210.2 0.0 all-gather.2.cloned.1.call-start
  210.2 0.6 copy-done.3
  210.9 259.8 %reduce-scatter.2.cloned.1.call-done = bf16[16,2304]{1,0:T(8,128)(2,1)} async-done(((bf16[512,2304]{1,0:T(8,128)(2,1)}), bf16[16,2304]{1,0:T(8,128)(2,1)}) %reduce-scatter.2.cloned.1.call-update) | async-done | bytes 73744 | tf_op jit(solution)/shard_map/reduce_scatter | solution.py:16
  470.7 1.5 fusion.12
  472.2 0.0 all-gather.2.cloned.1.call-update
  472.2 0.0 all-reduce.5.cloned.1.call-start
  472.3 86.9 %all-gather.2.cloned.1.call-done = bf16[512,2304]{1,0:T(8,128)(2,1)} async-done(((bf16[16,2304]{1,0:T(8,128)(2,1)}), bf16[512,2304]{1,0:T(8,128)(2,1)}) %all-gather.2.cloned.1.call-update) | async-done | bytes 2359312 | tf_op jit(solution)/shard_map/all_gather | solution.py:24
  559.2 7.0 %fusion.1 = f32[512,1024]{1,0:T(8,128)} fusion(bf16[512,2304]{1,0:T(8,128)(2,1)} %all-gather.2.cloned.1.call-done, bf16[1,1024,2304]{2,1,0:T(8,128)(2,1)} %param.9), kind=kOutput, calls=%fused_computation.2 | convolution fusion | flops 2415919104 | bytes 9175040 | tf_op jit(solution)/shard_map/dot_general | solution.py:29
  566.3 0.0 all-reduce.5.cloned.1.call-update
  566.3 1.6 copy-done.1
  567.9 6.0 fusion
  573.8 70.4 %all-reduce.5.cloned.1.call-done = f32[512,1024]{1,0:T(8,128)} async-done(((f32[512,1024]{1,0:T(8,128)}), f32[512,1024]{1,0:T(8,128)}) %all-reduce.5.cloned.1.call-update) | async-done | bytes 2097168 | tf_op jit(solution)/shard_map/psum | solution.py:34
  644.2 3.0 fusion.8
  (6 shorter events, 0.0 us)
Async XLA Ops:
  7.2 108.7 %copy-start = (bf16[288,1024]{1,0:T(8,128)(2,1)S(1)}, bf16[288,1024]{1,0:T(8,128)(2,1)}, u32[]{:S(2)}) copy-start(bf16[288,1024]{1,0:T(8,128)(2,1)} %param.7) | copy-start | bytes 1769476
  7.2 196.0 %all-reduce.3.cloned.1.call-start = ((), (), s32[]{:S(2)}) async-start(), calls=%async_computation.1 | async-start | bytes 4194304 | tf_op jit(solution)/shard_map/psum | solution.py:10
  115.9 87.2 %copy-start.4 = (f32[1024]{0:T(1024)S(1)}, f32[1024]{0:T(1024)}, u32[]{:S(2)}) copy-start(f32[1024]{0:T(1024)} %param.8) | copy-start | bytes 12292
  118.0 352.7 %reduce-scatter.2.cloned.1.call-start = ((), (), s32[]{:S(2)}) async-start(), calls=%async_computation.2 | async-start | bytes 2433024 | tf_op jit(solution)/shard_map/reduce_scatter | solution.py:16
  210.1 0.7 copy-start.3
  210.1 260.5 %copy-start.2 = (bf16[1,16,2304]{2,1,0:T(8,128)(2,1)S(1)}, bf16[1,16,2304]{2,1,0:T(8,128)(2,1)}, u32[]{:S(2)}) copy-start(bf16[1,16,2304]{2,1,0:T(8,128)(2,1)} %param.11) | copy-start | bytes 221188
  210.2 349.1 %all-gather.2.cloned.1.call-start = ((), (), s32[]{:S(2)}) async-start(), calls=%async_computation.3 | async-start | bytes 2433024 | tf_op jit(solution)/shard_map/all_gather | solution.py:24
  472.2 172.0 %all-reduce.5.cloned.1.call-start = ((), (), s32[]{:S(2)}) async-start(), calls=%async_computation.4 | async-start | bytes 4194304 | tf_op jit(solution)/shard_map/psum | solution.py:34
  566.3 1.6 copy-start.1
Sparse Core Ops, SparseCore 0:
  118.1 85.0 all-reduce.2
  210.3 260.3 reduce-scatter.1
  474.6 84.5 all-gather.1
  566.4 77.7 all-reduce.4
where the time goes:
time: 655 us; the launch traced here: 654 us
  waiting for transfers between devices  502 us (77%)
  blocking collectives  109 us (17%)
  matrix products  25.1 us (4%)
  between operations  13.8 us (2%)
    reduce_scatter x1, waiting for transfers between devices, body(): lax.psum_scatter(jnp.dot(picked, decoder, preferred_element_type=jnp.floa...  260 us
    all_gather x1, blocking collectives, body(): source_rows = lax.all_gather(source, 'feat', axis=0, tiled=True)  109 us
    all_gather x1, waiting for transfers between devices, body(): piece = lax.all_gather(residual, 'feat', axis=0, tiled=True)  86.9 us
    psum x1, waiting for transfers between devices, body(): preact = lax.psum(partial_input, 'layer')  85.1 us
    psum x1, waiting for transfers between devices, body(): summed = lax.psum(grad_total, 'layer')  70.4 us
  transfers between devices with their start and end apart: 4, of which 4 were waited for; matrix products, arithmetic and copies ran while one was open for 1% of the time, Pallas kernels for 0%

commit v1 on v0

v1 whole, which is shorter than its diff:
```python
import functools

import jax
import jax.numpy as jnp
from jax import lax
from jax.experimental import pallas as pl
from jax.experimental.pallas import tpu as pltpu
from jax.sharding import PartitionSpec as P

MESH = pl.DeviceIdType.MESH
F32 = jnp.float32
BF16 = jnp.bfloat16

D = 2304
HD = D // 2
NF = 1024
HF = NF // 2
KD = 288
KP = 384
CH = 256
TILES = ((0, 256), (256, 256), (512, 256), (768, 256), (1024, 128))


def dot(a, b):
    return jnp.dot(a, b, preferred_element_type=F32)


def dot_nt(a, b):
    return lax.dot_general(a, b, (((1,), (1,)), ((), ())), preferred_element_type=F32)


class Ids:
    def __init__(self):
        self.table = {}

    def __getitem__(self, name):
        return self.table.setdefault(name, len(self.table))


N_SEM = 200


def kernel(src_ref, encw_ref, bias_ref, decw_ref, dbias_ref, tgt_ref, eg_ref, dg_ref,
           srcb, wenc, w, tg, pown, xs, xr, zs, zr, act, feats, feat_t, src_t, fgr, egacc,
           rb, t1, t2, qs, qr, us, ur, res, stag, egout, ssem, rsem, lsem):
    layer = lax.axis_index("layer")
    feat = lax.axis_index("feat")
    core, zl = lax.rem(layer, 2), lax.div(layer, 2)
    zh = lax.rem(feat, 2)
    y = lax.rem(lax.div(feat, 2), 4)
    x = lax.div(feat, 8)

    def feat_of(xx, yy, zz):
        return (lax.rem(xx, 4) * 4 + lax.rem(yy, 4)) * 2 + zz

    def xy_dev(dx, dy):
        return {"layer": layer, "feat": feat_of(x + dx, y + dy, zh)}

    partner_z = {"layer": layer, "feat": feat_of(x, y, 1 - zh)}
    partner_c = {"layer": zl * 2 + 1 - core, "feat": feat}

    def z_dev(j):
        return {"layer": lax.rem(zl + j, 4) * 2 + core, "feat": feat}

    ids = Ids()
    pending = []

    def send(src, dst, name, dev):
        k = ids[name] if isinstance(name, (tuple, str)) else name
        copy = pltpu.make_async_remote_copy(
            src_ref=src, dst_ref=dst, send_sem=ssem.at[k], recv_sem=rsem.at[k],
            device_id=dev, device_id_type=MESH)
        copy.start()
        pending.append(copy)

    def recv(dst, name):
        k = ids[name] if isinstance(name, (tuple, str)) else name
        pltpu.make_async_remote_copy(
            src_ref=dst, dst_ref=dst, send_sem=ssem.at[k], recv_sem=rsem.at[k],
            device_id=partner_c, device_id_type=MESH).wait_recv()

    loads = {}

    def load(name, src, dst):
        loads[name] = pltpu.make_async_copy(src, dst, lsem.at[len(loads)])
        loads[name].start()

    for h in range(2):
        load(("e", h), encw_ref.at[:, pl.ds(h * HF, HF)], wenc.at[h, pl.ds(0, KD)])
    for h in range(2):
        load(("d", h), decw_ref.at[0, pl.ds(h * HF, HF)], w.at[h])

    barrier = pltpu.get_barrier_semaphore()
    peers = [xy_dev(dx, dy) for dx in range(4) for dy in range(4) if dx or dy]
    peers += [partner_z, partner_c] + [z_dev(j) for j in range(1, 4)]
    for dev in peers:
        pl.semaphore_signal(barrier, inc=1, device_id=dev, device_id_type=MESH)

    me = x * 4 + y
    zero = jnp.zeros((16, KP - KD), BF16)
    srcb[zh, me] = jnp.concatenate([src_ref[...], zero], axis=1)
    tg[zh] = tgt_ref[0]
    for h in range(2):
        wenc[h, pl.ds(KD, KP - KD)] = jnp.zeros((KP - KD, HF), BF16)
    pl.semaphore_wait(barrier, len(peers))

    for i in range(32):
        ids[("src", i)]
    send(srcb.at[zh, me], srcb.at[zh, me], zh * 16, partner_z)
    for dx in range(4):
        for dy in range(4):
            if dx or dy:
                send(srcb.at[zh, me], srcb.at[zh, me], zh * 16 + dx * 4 + dy, xy_dev(dx, dy))
    oz = 1 - zh
    recv(srcb.at[oz, me], oz * 16)
    for dx in range(4):
        for dy in range(4):
            if dx or dy:
                send(srcb.at[oz, me], srcb.at[oz, me], oz * 16 + dx * 4 + dy, xy_dev(dx, dy))
    send(tg.at[zh], tg.at[zh], "tgt", partner_z)

    def layer_sum_start(c, ph, half_of):
        xs[ph, c] = half_of(1 - core).astype(BF16)
        send(xs.at[ph, c], xr.at[ph, c], ("x", ph, c), partner_c)
        pown[c] = half_of(core)

    def layer_sum_z(c, ph):
        recv(xr.at[ph, c], ("x", ph, c))
        both = pown[c] + xr[ph, c].astype(F32)
        pown[c] = both
        zs[ph, c] = both.astype(BF16)
        for j in range(1, 4):
            to = lax.rem(zl + j, 4)
            send(zs.at[ph, c, pl.ds(to * 64, 64)], zr.at[ph, c, j - 1], ("z", ph, c, j), z_dev(j))

    def layer_sum_end(c, ph):
        total = pown[c, pl.ds(pl.multiple_of(zl * 64, 64), 64)]
        for j in range(1, 4):
            recv(zr.at[ph, c, j - 1], ("z", ph, c, j))
            total = total + zr[ph, c, j - 1].astype(F32)
        return total

    def share_start(c, ph, buf):
        mine = buf.at[c, core, zl]
        for j in range(1, 4):
            send(mine, mine, ("g", ph, c, j), z_dev(j))
        send(mine, mine, ("h", ph, c, 0), partner_c)

    def share_pass(c, ph, buf):
        for j in range(1, 4):
            at = buf.at[c, core, lax.rem(zl + 4 - j, 4)]
            recv(at, ("g", ph, c, j))
            send(at, at, ("h", ph, c, j), partner_c)

    def share_end(c, ph, buf):
        for j in range(4):
            recv(buf.at[c, 1 - core, lax.rem(zl + 4 - j, 4)], ("h", ph, c, j))

    def st_preact(c):
        for dx in range(4):
            for dy in range(4):
                if dx or dy:
                    p = lax.rem(x + 4 - dx, 4) * 4 + lax.rem(y + 4 - dy, 4)
                    recv(srcb.at[c, p], c * 16 + dx * 4 + dy)
        if c == 0:
            loads[("e", 0)].wait()
            loads[("e", 1)].wait()
        rows = srcb[c].reshape(CH, KP)
        layer_sum_start(c, 0, lambda h: dot(rows, wenc[h]))

    def st_preact_z(c):
        layer_sum_z(c, 0)

    def st_features(c):
        bias = bias_ref[pl.ds(core, 1), :]
        active = jnp.maximum(layer_sum_end(c, 0) + bias, 0.0)
        act[c] = active
        feats[c, core, zl] = (active * active).astype(BF16)
        share_start(c, 0, feats)

    def st_features_pass(c):
        share_pass(c, 0, feats)

    def axes(half):
        if half == 0:
            return x, y, (lambda da, db: xy_dev(da, db))
        return y, x, (lambda da, db: xy_dev(db, da))

    def sel(ref, half, c, a, b, nb):
        if half == 0:
            return ref.at[half, c, a, pl.ds(b, nb)]
        return ref.at[half, c, pl.ds(b, nb), a]

    def st_rebuilt(c):
        share_end(c, 0, feats)
        if c == 0:
            loads[("d", 0)].wait()
            loads[("d", 1)].wait()
        f0 = feats[c, 0].reshape(CH, HF)
        f1 = feats[c, 1].reshape(CH, HF)
        for half in range(2):
            for off, n in TILES:
                cols = pl.ds(half * HD + off, n)
                part = dot(f0, w[0, :, cols]) + dot(f1, w[1, :, cols])
                rb[half, c, :, :, :, pl.ds(off, n)] = part.astype(BF16).reshape(4, 4, 16, n)
            a, b, dev = axes(half)
            up, dn, op = lax.rem(a + 1, 4), lax.rem(a + 3, 4), lax.rem(a + 2, 4)
            send(sel(rb, half, c, op, 0, 2), t1.at[half, c, 0], ("r1", half, c, 0), dev(1, 0))
            send(sel(rb, half, c, op, 2, 2), t1.at[half, c, 1], ("r1", half, c, 1), dev(3, 0))
            send(sel(rb, half, c, up, 2, 2), t2.at[half, c, 0, pl.ds(2, 2)], ("r2", half, c, 0), dev(1, 0))
            send(sel(rb, half, c, dn, 0, 2), t2.at[half, c, 1, pl.ds(0, 2)], ("r2", half, c, 1), dev(3, 0))

    def st_transpose(c):
        for h in range(2):
            feat_t[h, :, pl.ds(c * CH, CH)] = feats[c, h].reshape(CH, HF).T

    def st_ring(c):
        for half in range(2):
            a, b, dev = axes(half)
            up, dn = lax.rem(a + 1, 4), lax.rem(a + 3, 4)
            recv(t1.at[half, c, 0], ("r1", half, c, 0))
            at = sel(rb, half, c, up, 0, 2)
            at[...] = (at[...].astype(F32) + t1[half, c, 0].astype(F32)).astype(BF16)
            send(at, t2.at[half, c, 0, pl.ds(0, 2)], ("r3", half, c, 0), dev(1, 0))
            recv(t1.at[half, c, 1], ("r1", half, c, 1))
            at = sel(rb, half, c, dn, 2, 2)
            at[...] = (at[...].astype(F32) + t1[half, c, 1].astype(F32)).astype(BF16)
            send(at, t2.at[half, c, 1, pl.ds(2, 2)], ("r3", half, c, 1), dev(3, 0))

    def st_second(c):
        for half in range(2):
            a, b, dev = axes(half)
            recv(t2.at[half, c, 0, pl.ds(2, 2)], ("r2", half, c, 0))
            recv(t2.at[half, c, 1, pl.ds(0, 2)], ("r2", half, c, 1))
            recv(t2.at[half, c, 0, pl.ds(0, 2)], ("r3", half, c, 0))
            recv(t2.at[half, c, 1, pl.ds(2, 2)], ("r3", half, c, 1))
            own = sel(rb, half, c, a, 0, 4)
            qs[half, c] = own[...].astype(F32) + t2[half, c, 0].astype(F32) + t2[half, c, 1].astype(F32)
            us[half, c] = qs[half, c].astype(BF16)
            for j in range(1, 4):
                send(us.at[half, c, lax.rem(b + j, 4)], qr.at[half, c, j - 1], ("q", half, c, j), dev(0, j))

    def st_swap(c):
        for half in range(2):
            a, b, dev = axes(half)
            total = qs[half, c, b]
            for j in range(1, 4):
                recv(qr.at[half, c, j - 1], ("q", half, c, j))
                total = total + qr[half, c, j - 1].astype(F32)
            us[half, c, b] = total.astype(BF16)
            send(us.at[half, c, b], ur.at[half, c], ("u", half, c), partner_z)

    def st_residual(c):
        if c == 0:
            recv(tg.at[oz], "tgt")
        for half in range(2):
            a, b, dev = axes(half)
            cols = pl.ds(half * HD, HD)
            recv(ur.at[half, c], ("u", half, c))
            total = us[half, c, b].astype(F32) + ur[half, c].astype(F32)
            total = total + dbias_ref[:, cols] - tg[c, :, cols].astype(F32)
            res[half, c, x, y] = total.astype(BF16)
            mine = res.at[half, c, x, y]
            for j in range(1, 4):
                send(mine, mine, ("a", half, c, j), dev(0, j))

    def st_gather(c):
        for half in range(2):
            a, b, dev = axes(half)
            for j in range(1, 4):
                at = (res.at[half, c, a, lax.rem(b + 4 - j, 4)] if half == 0
                      else res.at[half, c, lax.rem(b + 4 - j, 4), a])
                recv(at, ("a", half, c, j))
            lo, hi = sel(res, half, c, a, 0, 2), sel(res, half, c, a, 2, 2)
            send(lo, lo, ("b", half, c, 0), dev(1, 0))
            send(hi, hi, ("b", half, c, 1), dev(3, 0))
            send(hi, hi, ("b", half, c, 2), dev(1, 0))
            send(lo, lo, ("b", half, c, 3), dev(3, 0))

    def st_forward(c):
        for half in range(2):
            a, b, dev = axes(half)
            up, dn = lax.rem(a + 1, 4), lax.rem(a + 3, 4)
            at = sel(res, half, c, dn, 0, 2)
            recv(at, ("b", half, c, 0))
            send(at, at, ("f", half, c, 0), dev(1, 0))
            at = sel(res, half, c, up, 2, 2)
            recv(at, ("b", half, c, 1))
            send(at, at, ("f", half, c, 1), dev(3, 0))

    def st_summed(c):
        for half in range(2):
            a, b, dev = axes(half)
            up, dn, op = lax.rem(a + 1, 4), lax.rem(a + 3, 4), lax.rem(a + 2, 4)
            recv(sel(res, half, c, dn, 2, 2), ("b", half, c, 2))
            recv(sel(res, half, c, up, 0, 2), ("b", half, c, 3))
            recv(sel(res, half, c, op, 0, 2), ("f", half, c, 0))
            recv(sel(res, half, c, op, 2, 2), ("f", half, c, 1))

        def half_of(h):
            r0 = res[0, c].reshape(CH, HD)
            r1 = res[1, c].reshape(CH, HD)
            return jnp.concatenate(
                [dot_nt(r0, w[h, pl.ds(n, 256), pl.ds(0, HD)]) + dot_nt(r1, w[h, pl.ds(n, 256), pl.ds(HD, HD)])
                 for n in range(0, HF, 256)], axis=1)

        layer_sum_start(c, 1, half_of)

    def st_summed_z(c):
        layer_sum_z(c, 1)

    def st_fgrad(c):
        total = layer_sum_end(c, 1)
        fgr[c, core, zl] = (2.0 * act[c] * total).astype(BF16)
        share_start(c, 1, fgr)

    def st_fgrad_pass(c):
        share_pass(c, 1, fgr)

    def st_src_t(c):
        src_t[:, pl.ds(c * CH, CH)] = srcb[c].reshape(CH, KP).T

    def st_enc_grad(c):
        share_end(c, 1, fgr)
        lhs = src_t[:, pl.ds(c * CH, CH)]
        for h in range(2):
            part = dot(lhs, fgr[c, h].reshape(CH, HF))
            if c == 0:
                egacc[h] = part
            else:
                egout[:, pl.ds(h * HF, HF)] = (egacc[h] + part)[:KD].astype(BF16)

    outs = []

    def st_dec_grad(_):
        for h in range(2):
            for m in range(0, HF, 256):
                lhs = feat_t[h, pl.ds(m, 256), :]
                for half in range(2):
                    for off, n in TILES:
                        rhs = res[half, :, :, :, :, pl.ds(off, n)].reshape(2 * CH, n)
                        stag[pl.ds(h * HF + m, 256), pl.ds(half * HD + off, n)] = dot(lhs, rhs).astype(BF16)
                rows = pl.ds(h * HF + m, 256)
                copy = pltpu.make_async_copy(stag.at[rows], dg_ref.at[0, rows], lsem.at[4 + len(outs)])
                copy.start()
                outs.append(copy)

    order = [
        (st_preact, 0), (st_preact, 1), (st_preact_z, 0), (st_preact_z, 1), (st_features, 0), (st_features, 1),
        (st_features_pass, 0), (st_features_pass, 1), (st_rebuilt, 0), (st_rebuilt, 1), (st_transpose, 0), (st_ring, 0),
        (st_second, 0), (st_ring, 1), (st_swap, 0), (st_second, 1), (st_transpose, 1), (st_residual, 0), (st_swap, 1),
        (st_src_t, 0), (st_src_t, 1), (st_gather, 0), (st_residual, 1), (st_forward, 0), (st_gather, 1),
        (st_summed, 0), (st_forward, 1), (st_summed_z, 0), (st_summed, 1), (st_fgrad, 0), (st_summed_z, 1),
        (st_fgrad_pass, 0), (st_dec_grad, 0), (st_fgrad, 1), (st_enc_grad, 0), (st_fgrad_pass, 1), (st_enc_grad, 1),
    ]
    for stage, c in order:
        stage(c)
    copy = pltpu.make_async_copy(egout, eg_ref, lsem.at[4 + len(outs)])
    copy.start()
    outs.append(copy)
    for copy in pending:
        copy.wait_send()
    for copy in outs:
        copy.wait()
    assert len(ids.table) <= N_SEM


def step(source, enc_weight, enc_bias, dec_weight, dec_bias, targets):
    vmem = pl.BlockSpec(memory_space=pltpu.VMEM)
    hbm = pl.BlockSpec(memory_space=pl.ANY)
    V = pltpu.VMEM
    return pl.pallas_call(
        kernel,
        out_shape=(
            jax.ShapeDtypeStruct((KD, NF), BF16),
            jax.ShapeDtypeStruct((1, NF, D), BF16),
        ),
        in_specs=[vmem, hbm, vmem, hbm, vmem, vmem],
        out_specs=(hbm, hbm),
        scratch_shapes=[
            V((2, 16, 16, KP), BF16),
            V((2, KP, HF), BF16),
            V((2, HF, D), BF16),
            V((2, 16, D), BF16),
            V((2, CH, HF), F32),
            V((2, 2, CH, HF), BF16),
            V((2, 2, CH, HF), BF16),
            V((2, 2, CH, HF), BF16),
            V((2, 2, 3, 64, HF), BF16),
            V((2, 64, HF), F32),
            V((2, 2, 4, 64, HF), BF16),
            V((2, HF, 2 * CH), BF16),
            V((KP, 2 * CH), BF16),
            V((2, 2, 4, 64, HF), BF16),
            V((2, KP, HF), F32),
            V((2, 2, 4, 4, 16, HD), BF16),
            V((2, 2, 2, 2, 16, HD), BF16),
            V((2, 2, 2, 4, 16, HD), BF16),
            V((2, 2, 4, 16, HD), F32),
            V((2, 2, 3, 16, HD), BF16),
            V((2, 2, 4, 16, HD), BF16),
            V((2, 2, 16, HD), BF16),
            V((2, 2, 4, 4, 16, HD), BF16),
            V((NF, D), BF16),
            V((KD, NF), BF16),
            pltpu.SemaphoreType.DMA((N_SEM,)),
            pltpu.SemaphoreType.DMA((N_SEM,)),
            pltpu.SemaphoreType.DMA((16,)),
        ],
        compiler_params=pltpu.CompilerParams(
            collective_id=0, has_side_effects=True, vmem_limit_bytes=60 * 1024 * 1024),
    )(source, enc_weight, enc_bias.reshape(2, HF), dec_weight, dec_bias, targets)


def solution(mesh):
    placed = (
        P("feat", "layer"),
        P("layer", "feat"),
        P("feat"),
        P("layer", "feat", None),
        P("layer", None),
        P("layer", "feat", None),
    )
    return jax.shard_map(
        step,
        mesh=mesh,
        in_specs=placed,
        out_specs=(P("layer", "feat"), P("layer", "feat", None)),
        check_vma=False,
    )
```

time: 655 us -> 125 us (0.19)
  waiting for transfers between devices: 502 us -> 0 us
  Pallas kernels: 0 us -> 116 us
  blocking collectives: 109 us -> 0 us
  matrix products: 25.1 us -> 0 us
  between operations: 13.8 us -> 0.64 us
    reduce_scatter x1 -> x0, waiting for transfers between devices: 260 us -> none  [body(): lax.psum_scatter(jnp.dot(picked, decoder, preferred_element_type=jnp.floa...]
    psum x2 -> x0, waiting for transfers between devices: 155 us -> none  [the longest x1 85.1 us: body(): preact = lax.psum(partial_input, 'layer')]
    pallas_call x0 -> x1, Pallas kernels: none -> 116 us  [step(): pl.pallas_call(kernel, out_shape=(jax.ShapeDtypeStruct((KD, NF), BF16), j...]
    all_gather x1 -> x0, blocking collectives: 109 us -> none  [body(): source_rows = lax.all_gather(source, 'feat', axis=0, tiled=True)]
    all_gather x1 -> x0, waiting for transfers between devices: 86.9 us -> none  [body(): piece = lax.all_gather(residual, 'feat', axis=0, tiled=True)]
    dot_general x5 -> x0, matrix products: 25.1 us -> none  [the longest x1 7.05 us: body(): lax.dot_general(piece, decoder, (((1,), (1,)), ((), ())), preferred_eleme...]
  transfers between devices with their start and end apart: 4 -> 0, of which waited for: 4 -> 0; matrix products, arithmetic and copies ran while one was open for 1% -> 0% of each run, Pallas kernels for 0% -> 0%
where the time goes in v1:
time: 125 us
  Pallas kernels  116 us (93%)
  local copies, waits for them, and re-layouts  8.03 us (6%)
    pallas_call x1, Pallas kernels, step(): pl.pallas_call(kernel, out_shape=(jax.ShapeDtypeStruct((KD, NF), BF16), j...  116 us
    unnamed x2, local copies, waits for them, and re-layouts  6.74 us

profile of v1, /device:TPU:1, one launch (start us, length us, event | category | flops | bytes accessed | tf_op | source)
XLA Modules:
  0.0 125.1 jit_solution(10255978356975612759)
XLA Ops:
  0.6 1.3 %reshape.7.bias_ref = f32[2,512]{1,0:T(2,128)} reshape(f32[1024]{0:T(1024)} %param.8) | data formatting | bytes 8192 | tf_op jit(solution)/shard_map/reshape | solution.py:412
  1.9 116.4 %shard_map.77 = (bf16[288,1024]{1,0:T(8,128)(2,1)}, bf16[1,1024,2304]{2,1,0:T(8,128)(2,1)}) custom-call(bf16[16,288]{1,0:T(8,128)(2,1)} %src_ref.1, bf16[288,1024]{1,0:T(8,128)(2,1)} %encw_ref.1, f32[2,512]{1,0:T(2,128)} %reshape.7.bias_ref, bf16[1,1024,2304]{2,1,0:T(8,128)(2,1)} %decw_ref.1, f32[1,2304]{1,0:T(1,128)} %dbias_ref.1, bf16[1,16,2304]{2,1,0:T(8,128)(2,1)} %tgt_ref.1), custom_call_target="tpu_custom_call" | custom-call | tf_op jit(solution)/shard_map/pallas_call | solution.py:372
  118.4 1.9 %copy.10 = bf16[288,1024]{1,0:T(8,128)(2,1)} copy(bf16[288,1024]{1,0:T(8,128)(2,1)} %get-tuple-element.4) | data formatting | bytes 1179648
  120.3 4.8 %copy.11 = bf16[1,1024,2304]{2,1,0:T(8,128)(2,1)} copy(bf16[1,1024,2304]{2,1,0:T(8,128)(2,1)} %get-tuple-element.5) | data formatting | bytes 9437184

commit v2 on v1

v2 whole, which is shorter than its diff:
```python
import math

import jax
import jax.numpy as jnp
from jax import lax
from jax.experimental import pallas as pl
from jax.experimental.pallas import tpu as pltpu
from jax.sharding import PartitionSpec as P

MESH = pl.DeviceIdType.MESH
F32 = jnp.float32
BF16 = jnp.bfloat16

D = 2304
HD = D // 2
NF = 1024
HF = NF // 2
KD = 288
KP = 384
CH = 256
TILES = ((0, 256), (256, 256), (512, 256), (768, 256), (1024, 128))


def dot(a, b):
    return jnp.dot(a, b, preferred_element_type=F32)


def dot_nt(a, b):
    return lax.dot_general(a, b, (((1,), (1,)), ((), ())), preferred_element_type=F32)


class Ids:
    def __init__(self):
        self.table = {}

    def __getitem__(self, name):
        return self.table.setdefault(name, len(self.table))


N_RECV = 96
N_SEND = 31


def kernel(src_hbm, encw_ref, bias_hbm, decw_ref, dbias_hbm, tgt_hbm, eg_ref, dg_ref,
           src_ref, bias_ref, dbias_ref,
           srcb, wenc, w, tg, pown, acc, xs, xr, ls, nb, fb, act, feats, feat_t, src_t, fgr, egacc,
           rb, t1, t2, qs, qr, us, ur, res, rl, stag, egout, ssem, rsem, lsem):
    layer = lax.axis_index("layer")
    feat = lax.axis_index("feat")
    core, zl = lax.rem(layer, 2), lax.div(layer, 2)
    zh = lax.rem(feat, 2)
    y = lax.rem(lax.div(feat, 2), 4)
    x = lax.div(feat, 8)

    def feat_of(xx, yy, zz):
        return (lax.rem(xx, 4) * 4 + lax.rem(yy, 4)) * 2 + zz

    def xy_dev(dx, dy):
        return {"layer": layer, "feat": feat_of(x + dx, y + dy, zh)}

    partner_z = {"layer": layer, "feat": feat_of(x, y, 1 - zh)}
    partner_c = {"layer": zl * 2 + 1 - core, "feat": feat}

    def ring_dev(d):
        z = lax.rem(zh * 4 + zl + 8 + d, 8)
        return {"layer": lax.rem(z, 4) * 2 + core, "feat": feat_of(x, y, lax.div(z, 4))}

    ids, sids = Ids(), Ids()
    tiles, stage_tiles, now = {}, {}, ["start"]

    def bulk(n):
        wide = max(k for k in range(1, 19) if n % k == 0 and n // k <= 32)
        return w.at[0, pl.ds(0, n // wide * 16), pl.ds(0, wide * 128)]

    def count(ref):
        return math.prod(ref.shape) // 2048

    def send(src, dst, name, dev, slot=0, batch=None, tally=True):
        batch = batch or now[0]
        stage_tiles[batch] = stage_tiles.get(batch, 0) + count(src)
        if tally:
            tiles[name] = tiles.get(name, 0) + count(src)
        pltpu.make_async_remote_copy(
            src_ref=src, dst_ref=dst, send_sem=ssem.at[sids[batch]], recv_sem=rsem.at[ids[name] + slot],
            device_id=dev, device_id_type=MESH).start()

    def recv(name, slot=0, dst=None):
        if dst is None:
            dst = bulk(tiles[name])
        pltpu.make_async_copy(dst, dst, rsem.at[ids[name] + slot]).wait()

    loads = {}

    def load(name, src, dst):
        loads[name] = pltpu.make_async_copy(src, dst, lsem.at[len(loads)])
        loads[name].start()

    load("src", src_hbm, src_ref)
    load("tgt", tgt_hbm.at[0], tg.at[zh])
    load("bias", bias_hbm, bias_ref)
    load("dbias", dbias_hbm, dbias_ref)
    for h in range(2):
        load(("e", h), encw_ref.at[:, pl.ds(h * HF, HF)], wenc.at[h, pl.ds(0, KD)])
    for h in range(2):
        load(("d", h), decw_ref.at[0, pl.ds(h * HF, HF)], w.at[h])

    barrier = pltpu.get_barrier_semaphore()
    peers = [xy_dev(dx, dy) for dx in range(4) for dy in range(4) if dx or dy]
    peers += [partner_z, partner_c] + [ring_dev(d) for d in (1, -1, 3, -3)]
    for dev in peers:
        pl.semaphore_signal(barrier, inc=1, device_id=dev, device_id_type=MESH)

    me = x * 4 + y
    zero = jnp.zeros((16, KP - KD), BF16)
    loads['src'].wait()
    srcb[zh, me] = jnp.concatenate([src_ref[...], zero], axis=1)
    for h in range(2):
        wenc[h, pl.ds(KD, KP - KD)] = jnp.zeros((KP - KD, HF), BF16)
    pl.semaphore_wait(barrier, len(peers))

    for i in range(2):
        ids[("src", i)]
    oz = 1 - zh
    send(srcb.at[zh, me], srcb.at[zh, me], "srcz", partner_z)

    def spread(z, batch):
        for dx in range(4):
            for dy in range(4):
                if dx or dy:
                    send(srcb.at[z, me], srcb.at[z, me], ("src", 0), xy_dev(dx, dy), z, batch=batch)

    @pl.when(zh == 0)
    def _():
        spread(zh, "own")

    recv("srcz")
    now[0] = "relay"
    spread(oz, "relay")

    @pl.when(zh == 1)
    def _():
        spread(zh, "own")

    tiles[("src", 0)] //= 3
    stage_tiles["own"] //= 2
    for name in ("tgt", "bias", "dbias"):
        loads[name].wait()
    send(tg.at[zh], tg.at[zh], "tgt", partner_z)

    is_end = (zl == 0) | (zl == 3)
    is_inner = (zl == 1) | (zl == 2)
    toward = 1 - 2 * lax.div(zl, 2)
    far_dev = {"layer": lax.rem(zl + toward + 4, 4) * 2 + core, "feat": feat}
    near_dev = {"layer": lax.rem(zl - toward + 4, 4) * 2 + core, "feat": feat}

    def layer_sum_start(c, ph, half_of):
        xs[ph, c] = half_of(1 - core).astype(BF16)
        for b in range(4):
            rows = pl.ds(b * 64, 64)
            send(xs.at[ph, c, rows], xr.at[ph, c, rows], ("x", ph, c, b), partner_c)
        pown[c] = half_of(core)

    def line_start(c, ph, b):
        rows = pl.ds(b * 64, 64)
        recv(("x", ph, c, b))
        own = pown[c, rows] + xr[ph, c, rows].astype(F32)
        pown[c, rows] = own
        acc[c, rows] = own
        ids[("n", ph, c, b)], ids[("f", ph, c, b)]

        @pl.when(is_end)
        def _():
            ls[0, ph, c, rows] = own.astype(BF16)
            send(ls.at[0, ph, c, rows], nb.at[ph, c, rows], ("n", ph, c, b), far_dev, batch=("end", ph, c))

    def line_near(c, ph, b):
        rows = pl.ds(b * 64, 64)

        @pl.when(is_inner)
        def _():
            recv(("n", ph, c, b), dst=nb.at[ph, c, rows])
            both = acc[c, rows] + nb[ph, c, rows].astype(F32)
            acc[c, rows] = both
            ls[0, ph, c, rows] = both.astype(BF16)
            send(ls.at[0, ph, c, rows], fb.at[ph, c, rows], ("f", ph, c, b), far_dev, batch=("inner", ph, c))

    def line_far(c, ph, b, inner):
        rows = pl.ds(b * 64, 64)
        batch = ("inner" if inner else "end", ph, c)

        @pl.when(is_inner if inner else is_end)
        def _():
            recv(("f", ph, c, b), dst=fb.at[ph, c, rows])
            beyond = fb[ph, c, rows].astype(F32)
            if inner:
                ls[1, ph, c, rows] = (pown[c, rows] + beyond).astype(BF16)
                send(ls.at[1, ph, c, rows], fb.at[ph, c, rows], ("f", ph, c, b), near_dev, batch=batch)
            total = acc[c, rows] + beyond
            if ph == 0:
                bias = bias_ref[:, pl.ds(pl.multiple_of(core * HF, HF), HF)]
                active = jnp.maximum(total + bias, 0.0)
                act[c, rows] = active
                feats[c, core, b] = (active * active).astype(BF16)
                mine = feats.at[c, core, b]
            else:
                fgr[c, core, b] = (2.0 * act[c, rows] * total).astype(BF16)
                mine = fgr.at[c, core, b]
            send(mine, mine, ("h", ph, c), partner_c, batch=batch, tally=inner)

    def st_preact(c):
        recv(("src", 0), c)
        if c == 0:
            loads[("e", 0)].wait()
            loads[("e", 1)].wait()
        rows = srcb[c].reshape(CH, KP)
        layer_sum_start(c, 0, lambda h: dot(rows, wenc[h]))

    def st_line(c, ph, b):
        line_start(c, ph, b)

    def st_near(c, ph, b):
        line_near(c, ph, b)

    def st_far(c, ph, b):
        line_far(c, ph, b, True)

    def st_far_end(c, ph, b):
        line_far(c, ph, b, False)

    def axes(half):
        if half == 0:
            return x, y, (lambda da, db: xy_dev(da, db))
        return y, x, (lambda da, db: xy_dev(db, da))

    def sel(ref, half, c, a, b, nb):
        if half == 0:
            return ref.at[half, c, a, pl.ds(b, nb)]
        return ref.at[half, c, pl.ds(b, nb), a]

    def st_rebuilt(c):
        recv(("h", 0, c))
        if c == 0:
            loads[("d", 0)].wait()
            loads[("d", 1)].wait()
        f0 = feats[c, 0].reshape(CH, HF)
        f1 = feats[c, 1].reshape(CH, HF)
        for half in range(2):
            for off, n in TILES:
                cols = pl.ds(half * HD + off, n)
                part = dot(f0, w[0, :, cols]) + dot(f1, w[1, :, cols])
                rb[half, c, :, :, :, pl.ds(off, n)] = part.astype(BF16).reshape(4, 4, 16, n)
            a, b, dev = axes(half)
            up, dn, op = lax.rem(a + 1, 4), lax.rem(a + 3, 4), lax.rem(a + 2, 4)
            send(sel(rb, half, c, op, 0, 2), t1.at[half, c, 0], ("r1", half, c, 0), dev(1, 0))
            send(sel(rb, half, c, op, 2, 2), t1.at[half, c, 1], ("r1", half, c, 1), dev(3, 0))
            send(sel(rb, half, c, up, 2, 2), t2.at[half, c, 0, pl.ds(2, 2)], ("t2", half, c), dev(1, 0))
            send(sel(rb, half, c, dn, 0, 2), t2.at[half, c, 1, pl.ds(0, 2)], ("t2", half, c), dev(3, 0))

    def st_transpose(c):
        for h in range(2):
            feat_t[h, :, pl.ds(c * CH, CH)] = feats[c, h].reshape(CH, HF).T

    def st_ring(c):
        for half in range(2):
            a, b, dev = axes(half)
            up, dn = lax.rem(a + 1, 4), lax.rem(a + 3, 4)
            recv(("r1", half, c, 0))
            at = sel(rb, half, c, up, 0, 2)
            at[...] = (at[...].astype(F32) + t1[half, c, 0].astype(F32)).astype(BF16)
            send(at, t2.at[half, c, 0, pl.ds(0, 2)], ("t2", half, c), dev(1, 0))
            recv(("r1", half, c, 1))
            at = sel(rb, half, c, dn, 2, 2)
            at[...] = (at[...].astype(F32) + t1[half, c, 1].astype(F32)).astype(BF16)
            send(at, t2.at[half, c, 1, pl.ds(2, 2)], ("t2", half, c), dev(3, 0))

    def st_second(c):
        for half in range(2):
            a, b, dev = axes(half)
            recv(("t2", half, c))
            own = sel(rb, half, c, a, 0, 4)
            qs[half, c] = own[...].astype(F32) + t2[half, c, 0].astype(F32) + t2[half, c, 1].astype(F32)
            us[half, c] = qs[half, c].astype(BF16)
            for j in range(1, 4):
                send(us.at[half, c, lax.rem(b + j, 4)], qr.at[half, c, j - 1], ("q", half, c), dev(0, j))

    def st_swap(c):
        for half in range(2):
            a, b, dev = axes(half)
            total = qs[half, c, b]
            recv(("q", half, c))
            for j in range(1, 4):
                total = total + qr[half, c, j - 1].astype(F32)
            us[half, c, b] = total.astype(BF16)
            send(us.at[half, c, b], rl.at[half, c], ("v", half, c), ring_dev(1 - 2 * half))

    def st_swap_pass(c):
        for half in range(2):
            recv(("v", half, c))
            send(rl.at[half, c], ur.at[half, c], ("u", half, c), ring_dev(3 - 6 * half))

    def st_residual(c):
        if c == 0:
            recv("tgt")
        for half in range(2):
            a, b, dev = axes(half)
            cols = pl.ds(half * HD, HD)
            recv(("u", half, c))
            total = us[half, c, b].astype(F32) + ur[half, c].astype(F32)
            total = total + dbias_ref[:, cols] - tg[c, :, cols].astype(F32)
            res[half, c, x, y] = total.astype(BF16)
            mine = res.at[half, c, x, y]
            for j in range(1, 4):
                send(mine, mine, ("a", half, c), dev(0, j))

    def st_gather(c):
        for half in range(2):
            a, b, dev = axes(half)
            recv(("a", half, c))
            lo, hi = sel(res, half, c, a, 0, 2), sel(res, half, c, a, 2, 2)
            send(lo, lo, ("b", half, c, 0), dev(1, 0))
            send(hi, hi, ("b", half, c, 1), dev(3, 0))
            send(hi, hi, ("e", half, c), dev(1, 0))
            send(lo, lo, ("e", half, c), dev(3, 0))

    def st_forward(c):
        for half in range(2):
            a, b, dev = axes(half)
            up, dn = lax.rem(a + 1, 4), lax.rem(a + 3, 4)
            at = sel(res, half, c, dn, 0, 2)
            recv(("b", half, c, 0))
            send(at, at, ("e", half, c), dev(1, 0))
            at = sel(res, half, c, up, 2, 2)
            recv(("b", half, c, 1))
            send(at, at, ("e", half, c), dev(3, 0))

    def st_summed(c):
        for half in range(2):
            recv(("e", half, c))

        def half_of(h):
            r0 = res[0, c].reshape(CH, HD)
            r1 = res[1, c].reshape(CH, HD)
            return jnp.concatenate(
                [dot_nt(r0, w[h, pl.ds(n, 256), pl.ds(0, HD)]) + dot_nt(r1, w[h, pl.ds(n, 256), pl.ds(HD, HD)])
                 for n in range(0, HF, 256)], axis=1)

        layer_sum_start(c, 1, half_of)

    def st_src_t(c):
        src_t[:, pl.ds(c * CH, CH)] = srcb[c].reshape(CH, KP).T

    def st_enc_grad(c):
        recv(("h", 1, c))
        lhs = src_t[:, pl.ds(c * CH, CH)]
        for h in range(2):
            part = dot(lhs, fgr[c, h].reshape(CH, HF))
            if c == 0:
                egacc[h] = part
            else:
                egout[:, pl.ds(h * HF, HF)] = (egacc[h] + part)[:KD].astype(BF16)

    outs = []

    def put(src, dst):
        outs.append(pltpu.make_async_copy(src, dst, lsem.at[8 + len(outs)]))
        outs[-1].start()

    def st_dec_grad(h):
        for m in range(0, HF, 256):
            lhs = feat_t[h, pl.ds(m, 256), :]
            for half in range(2):
                for off, n in TILES:
                    rhs = res[half, :, :, :, :, pl.ds(off, n)].reshape(2 * CH, n)
                    stag[pl.ds(h * HF + m, 256), pl.ds(half * HD + off, n)] = dot(lhs, rhs).astype(BF16)
            rows = pl.ds(h * HF + m, 256)
            put(stag.at[rows], dg_ref.at[0, rows])

    def line(c, ph):
        return [(st_line, c, ph, b) for b in range(4)]

    def near(c, ph, *bs):
        return [(st_near, c, ph, b) for b in bs]

    def far(c, ph, *bs):
        return [(st_far, c, ph, b) for b in bs]

    def end(c, ph):
        return [(st_far_end, c, ph, b) for b in range(4)]

    order = [
        (st_preact, 0), *line(0, 0), (st_preact, 1), *line(1, 0),
        *near(0, 0, 0, 1, 2), *far(0, 0, 0), *near(0, 0, 3), *far(0, 0, 1), *near(1, 0, 0), *far(0, 0, 2),
        *near(1, 0, 1), *far(0, 0, 3), *near(1, 0, 2, 3), *end(0, 0),
        (st_rebuilt, 0), *far(1, 0, 0, 1, 2, 3), *end(1, 0), (st_ring, 0), (st_transpose, 0), (st_src_t, 0), (st_src_t, 1),
        (st_second, 0), (st_rebuilt, 1), (st_swap, 0), (st_transpose, 1), (st_ring, 1), (st_swap_pass, 0), (st_second, 1),
        (st_residual, 0), (st_swap, 1), (st_gather, 0), (st_swap_pass, 1), (st_forward, 0), (st_residual, 1),
        (st_summed, 0), *line(0, 1), (st_gather, 1),
        *near(0, 1, 0, 1), (st_forward, 1), *near(0, 1, 2), *far(0, 1, 0), *near(0, 1, 3), *far(0, 1, 1, 2, 3),
        (st_summed, 1), *line(1, 1), *end(0, 1), (st_dec_grad, 0),
        *near(1, 1, 0, 1, 2), *far(1, 1, 0), *near(1, 1, 3), *far(1, 1, 1, 2, 3),
        (st_dec_grad, 1), (st_enc_grad, 0), *end(1, 1), (st_enc_grad, 1),
    ]
    for stage, *args in order:
        now[0] = (stage.__name__, *args)
        stage(*args)
    put(egout, eg_ref)
    for batch, n in stage_tiles.items():
        if batch[0] in ("end", "inner"):
            @pl.when(is_end if batch[0] == "end" else is_inner)
            def _():
                pltpu.make_async_copy(bulk(n), bulk(n), ssem.at[sids[batch]]).wait()
        else:
            pltpu.make_async_copy(bulk(n), bulk(n), ssem.at[sids[batch]]).wait()
    for copy in outs:
        copy.wait()
    assert len(ids.table) == N_RECV and len(sids.table) == N_SEND, (len(ids.table), len(sids.table))


def step(source, enc_weight, enc_bias, dec_weight, dec_bias, targets):
    vmem = pl.BlockSpec(memory_space=pltpu.VMEM)
    hbm = pl.BlockSpec(memory_space=pltpu.HBM)
    V = pltpu.VMEM
    return pl.pallas_call(
        kernel,
        out_shape=(
            jax.ShapeDtypeStruct((KD, NF), BF16),
            jax.ShapeDtypeStruct((1, NF, D), BF16),
        ),
        in_specs=[hbm] * 6,
        out_specs=(pl.BlockSpec(memory_space=pl.ANY),) * 2,
        scratch_shapes=[
            V((16, KD), BF16),
            V((1, NF), F32),
            V((1, D), F32),
            V((2, 16, 16, KP), BF16),
            V((2, KP, HF), BF16),
            V((2, HF, D), BF16),
            V((2, 16, D), BF16),
            V((2, CH, HF), F32),
            V((2, CH, HF), F32),
            V((2, 2, CH, HF), BF16),
            V((2, 2, CH, HF), BF16),
            V((2, 2, 2, CH, HF), BF16),
            V((2, 2, CH, HF), BF16),
            V((2, 2, CH, HF), BF16),
            V((2, CH, HF), F32),
            V((2, 2, 4, 64, HF), BF16),
            V((2, HF, 2 * CH), BF16),
            V((KP, 2 * CH), BF16),
            V((2, 2, 4, 64, HF), BF16),
            V((2, KP, HF), F32),
            V((2, 2, 4, 4, 16, HD), BF16),
            V((2, 2, 2, 2, 16, HD), BF16),
            V((2, 2, 2, 4, 16, HD), BF16),
            V((2, 2, 4, 16, HD), F32),
            V((2, 2, 3, 16, HD), BF16),
            V((2, 2, 4, 16, HD), BF16),
            V((2, 2, 16, HD), BF16),
            V((2, 2, 4, 4, 16, HD), BF16),
            V((2, 2, 16, HD), BF16),
            V((NF, D), BF16),
            V((KD, NF), BF16),
            pltpu.SemaphoreType.DMA((N_SEND,)),
            pltpu.SemaphoreType.DMA((N_RECV,)),
            pltpu.SemaphoreType.DMA((13,)),
        ],
        compiler_params=pltpu.CompilerParams(
            collective_id=0, has_side_effects=True, vmem_limit_bytes=48 * 1024 * 1024),
    )(*[pltpu.with_memory_space_constraint(a, pltpu.HBM)
        for a in (source, enc_weight, enc_bias.reshape(1, NF), dec_weight, dec_bias, targets)])


def solution(mesh):
    placed = (
        P("feat", "layer"),
        P("layer", "feat"),
        P("feat"),
        P("layer", "feat", None),
        P("layer", None),
        P("layer", "feat", None),
    )
    return jax.shard_map(
        step,
        mesh=mesh,
        in_specs=placed,
        out_specs=(P("layer", "feat"), P("layer", "feat", None)),
        check_vma=False,
    )
```

time: 125 us -> 109 us (0.87)
  Pallas kernels: 116 us -> 106 us
  local copies, waits for them, and re-layouts: 8.03 us -> 3 us
    pallas_call x1, Pallas kernels: 116 us -> 106 us  [step(): pl.pallas_call(kernel, out_shape=(jax.ShapeDtypeStruct((KD, NF), BF16), j...]
    unnamed x2, local copies, waits for them, and re-layouts: 6.74 us -> 3 us
    reshape x1 -> x0, local copies, waits for them, and re-layouts: 1.29 us -> none  [step(): enc_bias.reshape(2, HF)]
where the time goes in v2:
time: 109 us
  Pallas kernels  106 us (97%)
  local copies, waits for them, and re-layouts  3 us (3%)
    pallas_call x1, Pallas kernels, step(): pl.pallas_call(kernel, out_shape=(jax.ShapeDtypeStruct((KD, NF), BF16), j...  106 us
    unnamed x2, local copies, waits for them, and re-layouts  3 us

profile of v2, /device:TPU:1, one launch (start us, length us, event | category | flops | bytes accessed | tf_op | source)
XLA Modules:
  0.0 109.3 jit_solution(12210383545781716936)
XLA Ops:
  0.6 105.7 %shard_map.77 = (bf16[288,1024]{1,0:T(8,128)(2,1)S(1)}, bf16[1,1024,2304]{2,1,0:T(8,128)(2,1)S(1)}) custom-call(bf16[16,288]{1,0:T(8,128)(2,1)} %src_hbm.1, bf16[288,1024]{1,0:T(8,128)(2,1)} %encw_ref.1, f32[1,1024]{1,0:T(1,128)} %bitcast.1, bf16[1,1024,2304]{2,1,0:T(8,128)(2,1)} %decw_ref.1, f32[1,2304]{1,0:T(1,128)} %dbias_hbm.1, bf16[1,16,2304]{2,1,0:T(8,128)(2,1)} %tgt_hbm.1), custom_call_target="tpu_custom_call" | custom-call | tf_op jit(solution)/shard_map/pallas_call | solution.py:423
  106.3 0.8 copy.10
  107.1 2.2 %copy.11 = bf16[1,1024,2304]{2,1,0:T(8,128)(2,1)} copy(bf16[1,1024,2304]{2,1,0:T(8,128)(2,1)S(1)} %get-tuple-element.5) | data formatting | bytes 9437184

commit v3 on v2

--- a/solution.py
+++ b/solution.py
@@ -18,6 +18,10 @@
 KD = 288
 KP = 384
 CH = 256
+GW = 384
+NG = HD // GW
+NB = 8
+RB = CH // NB
 TILES = ((0, 256), (256, 256), (512, 256), (768, 256), (1024, 128))
 
 
@@ -37,13 +41,13 @@
         return self.table.setdefault(name, len(self.table))
 
 
-N_RECV = 96
-N_SEND = 31
+N_RECV = 122
+N_SEND = 29
 
 
 def kernel(src_hbm, encw_ref, bias_hbm, decw_ref, dbias_hbm, tgt_hbm, eg_ref, dg_ref,
            src_ref, bias_ref, dbias_ref,
-           srcb, wenc, w, tg, pown, acc, xs, xr, ls, nb, fb, act, feats, feat_t, src_t, fgr, egacc,
+           srcb, wenc, w, tg, pown, acc, xacc, xs, xr, ls, nb, fb, act, feats, feat_t, src_t, fgr, egacc,
            rb, t1, t2, qs, qr, us, ur, res, rl, stag, egout, ssem, rsem, lsem):
     layer = lax.axis_index("layer")
     feat = lax.axis_index("feat")
@@ -153,16 +157,20 @@
     far_dev = {"layer": lax.rem(zl + toward + 4, 4) * 2 + core, "feat": feat}
     near_dev = {"layer": lax.rem(zl - toward + 4, 4) * 2 + core, "feat": feat}
 
+    def share_x(c, ph):
+        for b in range(2):
+            rows = pl.ds(b * 128, 128)
+            send(xs.at[ph, c, rows], xr.at[ph, c, rows], ("x", ph, c, b), partner_c)
+
     def layer_sum_start(c, ph, half_of):
         xs[ph, c] = half_of(1 - core).astype(BF16)
-        for b in range(4):
-            rows = pl.ds(b * 64, 64)
-            send(xs.at[ph, c, rows], xr.at[ph, c, rows], ("x", ph, c, b), partner_c)
+        share_x(c, ph)
         pown[c] = half_of(core)
 
     def line_start(c, ph, b):
-        rows = pl.ds(b * 64, 64)
-        recv(("x", ph, c, b))
+        rows = pl.ds(b * RB, RB)
+        if b % (NB // 2) == 0:
+            recv(("x", ph, c, b // (NB // 2)))
         own = pown[c, rows] + xr[ph, c, rows].astype(F32)
         pown[c, rows] = own
         acc[c, rows] = own
@@ -174,7 +182,7 @@
             send(ls.at[0, ph, c, rows], nb.at[ph, c, rows], ("n", ph, c, b), far_dev, batch=("end", ph, c))
 
     def line_near(c, ph, b):
-        rows = pl.ds(b * 64, 64)
+        rows = pl.ds(b * RB, RB)
 
         @pl.when(is_inner)
         def _():
@@ -185,7 +193,7 @@
             send(ls.at[0, ph, c, rows], fb.at[ph, c, rows], ("f", ph, c, b), far_dev, batch=("inner", ph, c))
 
     def line_far(c, ph, b, inner):
-        rows = pl.ds(b * 64, 64)
+        rows = pl.ds(b * RB, RB)
         batch = ("inner" if inner else "end", ph, c)
 
         @pl.when(is_inner if inner else is_end)
@@ -207,13 +215,13 @@
                 mine = fgr.at[c, core, b]
             send(mine, mine, ("h", ph, c), partner_c, batch=batch, tally=inner)
 
-    def st_preact(c):
-        recv(("src", 0), c)
-        if c == 0:
+    def st_preact(k):
+        recv(("src", 0), k)
+        if k == 0:
             loads[("e", 0)].wait()
             loads[("e", 1)].wait()
-        rows = srcb[c].reshape(CH, KP)
-        layer_sum_start(c, 0, lambda h: dot(rows, wenc[h]))
+        rows = srcb[k].reshape(CH, KP)
+        layer_sum_start(k, 0, lambda h: dot(rows, wenc[h]))
 
     def st_line(c, ph, b):
         line_start(c, ph, b)
@@ -232,119 +240,134 @@
             return x, y, (lambda da, db: xy_dev(da, db))
         return y, x, (lambda da, db: xy_dev(db, da))
 
-    def sel(ref, half, c, a, b, nb):
+    def sel(ref, half, c, a, b, nb, cols):
         if half == 0:
-            return ref.at[half, c, a, pl.ds(b, nb)]
-        return ref.at[half, c, pl.ds(b, nb), a]
-
-    def st_rebuilt(c):
-        recv(("h", 0, c))
-        if c == 0:
+            return ref.at[half, c, a, pl.ds(b, nb), :, cols]
+        return ref.at[half, c, pl.ds(b, nb), a, :, cols]
+
+    def group(g):
+        return pl.ds(g * GW, GW)
+
+    def st_rebuilt(c, g):
+        if g == 0:
+            recv(("h", 0, c))
+        if g == 0 and c == 0:
             loads[("d", 0)].wait()
             loads[("d", 1)].wait()
         f0 = feats[c, 0].reshape(CH, HF)
         f1 = feats[c, 1].reshape(CH, HF)
-        for half in range(2):
-            for off, n in TILES:
+        cg = group(g)
+        for half in range(2):
+            for off, n in ((0, 256), (256, 128)):
+                off = g * GW + off
                 cols = pl.ds(half * HD + off, n)
                 part = dot(f0, w[0, :, cols]) + dot(f1, w[1, :, cols])
                 rb[half, c, :, :, :, pl.ds(off, n)] = part.astype(BF16).reshape(4, 4, 16, n)
             a, b, dev = axes(half)
             up, dn, op = lax.rem(a + 1, 4), lax.rem(a + 3, 4), lax.rem(a + 2, 4)
-            send(sel(rb, half, c, op, 0, 2), t1.at[half, c, 0], ("r1", half, c, 0), dev(1, 0))
-            send(sel(rb, half, c, op, 2, 2), t1.at[half, c, 1], ("r1", half, c, 1), dev(3, 0))
-            send(sel(rb, half, c, up, 2, 2), t2.at[half, c, 0, pl.ds(2, 2)], ("t2", half, c), dev(1, 0))
-            send(sel(rb, half, c, dn, 0, 2), t2.at[half, c, 1, pl.ds(0, 2)], ("t2", half, c), dev(3, 0))
+            send(sel(rb, half, c, op, 0, 2, cg), t1.at[half, c, 0, :, :, cg], ("r", c, g), dev(1, 0))
+            send(sel(rb, half, c, op, 2, 2, cg), t1.at[half, c, 1, :, :, cg], ("r", c, g), dev(3, 0))
+            send(sel(rb, half, c, up, 2, 2, cg), t2.at[half, c, 0, pl.ds(2, 2), :, cg], ("t", c, g), dev(1, 0))
+            send(sel(rb, half, c, dn, 0, 2, cg), t2.at[half, c, 1, pl.ds(0, 2), :, cg], ("t", c, g), dev(3, 0))
 
     def st_transpose(c):
         for h in range(2):
             feat_t[h, :, pl.ds(c * CH, CH)] = feats[c, h].reshape(CH, HF).T
 
-    def st_ring(c):
+    def st_ring(c, g):
+        cg = group(g)
+        recv(("r", c, g))
         for half in range(2):
             a, b, dev = axes(half)
             up, dn = lax.rem(a + 1, 4), lax.rem(a + 3, 4)
-            recv(("r1", half, c, 0))
-            at = sel(rb, half, c, up, 0, 2)
-            at[...] = (at[...].astype(F32) + t1[half, c, 0].astype(F32)).astype(BF16)
-            send(at, t2.at[half, c, 0, pl.ds(0, 2)], ("t2", half, c), dev(1, 0))
-            recv(("r1", half, c, 1))
-            at = sel(rb, half, c, dn, 2, 2)
-            at[...] = (at[...].astype(F32) + t1[half, c, 1].astype(F32)).astype(BF16)
-            send(at, t2.at[half, c, 1, pl.ds(2, 2)], ("t2", half, c), dev(3, 0))
-
-    def st_second(c):
-        for half in range(2):
-            a, b, dev = axes(half)
-            recv(("t2", half, c))
-            own = sel(rb, half, c, a, 0, 4)
-            qs[half, c] = own[...].astype(F32) + t2[half, c, 0].astype(F32) + t2[half, c, 1].astype(F32)
-            us[half, c] = qs[half, c].astype(BF16)
+            at = sel(rb, half, c, up, 0, 2, cg)
+            at[...] = (at[...].astype(F32) + t1[half, c, 0, :, :, cg].astype(F32)).astype(BF16)
+            send(at, t2.at[half, c, 0, pl.ds(0, 2), :, cg], ("t", c, g), dev(1, 0))
+            at = sel(rb, half, c, dn, 2, 2, cg)
+            at[...] = (at[...].astype(F32) + t1[half, c, 1, :, :, cg].astype(F32)).astype(BF16)
+            send(at, t2.at[half, c, 1, pl.ds(2, 2), :, cg], ("t", c, g), dev(3, 0))
+
+    def st_second(c, g):
+        cg = group(g)
+        recv(("t", c, g))
+        for half in range(2):
+            a, b, dev = axes(half)
+            own = sel(rb, half, c, a, 0, 4, cg)
+            total = (own[...].astype(F32) + t2[half, c, 0, :, :, cg].astype(F32)
+                     + t2[half, c, 1, :, :, cg].astype(F32))
+            qs[half, c, :, :, cg] = total
+            us[half, c, :, :, cg] = total.astype(BF16)
             for j in range(1, 4):
-                send(us.at[half, c, lax.rem(b + j, 4)], qr.at[half, c, j - 1], ("q", half, c), dev(0, j))
-
-    def st_swap(c):
-        for half in range(2):
-            a, b, dev = axes(half)
-            total = qs[half, c, b]
-            recv(("q", half, c))
+                send(us.at[half, c, lax.rem(b + j, 4), :, cg], qr.at[half, c, j - 1, :, cg], ("q", c, g), dev(0, j))
+
+    def st_swap(c, g):
+        cg = group(g)
+        recv(("q", c, g))
+        for half in range(2):
+            a, b, dev = axes(half)
+            total = qs[half, c, b, :, cg]
             for j in range(1, 4):
-                total = total + qr[half, c, j - 1].astype(F32)
-            us[half, c, b] = total.astype(BF16)
-            send(us.at[half, c, b], rl.at[half, c], ("v", half, c), ring_dev(1 - 2 * half))
-
-    def st_swap_pass(c):
-        for half in range(2):
-            recv(("v", half, c))
-            send(rl.at[half, c], ur.at[half, c], ("u", half, c), ring_dev(3 - 6 * half))
-
-    def st_residual(c):
-        if c == 0:
+                total = total + qr[half, c, j - 1, :, cg].astype(F32)
+            us[half, c, b, :, cg] = total.astype(BF16)
+            send(us.at[half, c, b, :, cg], ur.at[half, c, :, cg], ("u", c, g), partner_z)
+
+    def st_residual(c, g):
+        cg = group(g)
+        if c == 0 and g == 0:
             recv("tgt")
-        for half in range(2):
-            a, b, dev = axes(half)
-            cols = pl.ds(half * HD, HD)
-            recv(("u", half, c))
-            total = us[half, c, b].astype(F32) + ur[half, c].astype(F32)
+        recv(("u", c, g))
+        for half in range(2):
+            a, b, dev = axes(half)
+            cols = pl.ds(half * HD + g * GW, GW)
+            total = us[half, c, b, :, cg].astype(F32) + ur[half, c, :, cg].astype(F32)
             total = total + dbias_ref[:, cols] - tg[c, :, cols].astype(F32)
-            res[half, c, x, y] = total.astype(BF16)
-            mine = res.at[half, c, x, y]
+            res[half, c, x, y, :, cg] = total.astype(BF16)
+            mine = res.at[half, c, x, y, :, cg]
             for j in range(1, 4):
-                send(mine, mine, ("a", half, c), dev(0, j))
-
-    def st_gather(c):
-        for half in range(2):
-            a, b, dev = axes(half)
-            recv(("a", half, c))
-            lo, hi = sel(res, half, c, a, 0, 2), sel(res, half, c, a, 2, 2)
-            send(lo, lo, ("b", half, c, 0), dev(1, 0))
-            send(hi, hi, ("b", half, c, 1), dev(3, 0))
-            send(hi, hi, ("e", half, c), dev(1, 0))
-            send(lo, lo, ("e", half, c), dev(3, 0))
-
-    def st_forward(c):
+                send(mine, mine, ("a", c, g), dev(0, j))
+
+    def st_gather(c, g):
+        cg = group(g)
+        recv(("a", c, g))
+        for half in range(2):
+            a, b, dev = axes(half)
+            lo, hi = sel(res, half, c, a, 0, 2, cg), sel(res, half, c, a, 2, 2, cg)
+            send(lo, lo, ("b", c, g), dev(1, 0))
+            send(hi, hi, ("b", c, g), dev(3, 0))
+            send(hi, hi, ("e", c, g), dev(1, 0))
+            send(lo, lo, ("e", c, g), dev(3, 0))
+
+    def st_forward(c, g):
+        cg = group(g)
+        recv(("b", c, g))
         for half in range(2):
             a, b, dev = axes(half)
             up, dn = lax.rem(a + 1, 4), lax.rem(a + 3, 4)
-            at = sel(res, half, c, dn, 0, 2)
-            recv(("b", half, c, 0))
-            send(at, at, ("e", half, c), dev(1, 0))
-            at = sel(res, half, c, up, 2, 2)
-            recv(("b", half, c, 1))
-            send(at, at, ("e", half, c), dev(3, 0))
-
-    def st_summed(c):
-        for half in range(2):
-            recv(("e", half, c))
+            at = sel(res, half, c, dn, 0, 2, cg)
+            send(at, at, ("e", c, g), dev(1, 0))
+            at = sel(res, half, c, up, 2, 2, cg)
+            send(at, at, ("e", c, g), dev(3, 0))
+
+    def st_summed(c, g):
+        recv(("e", c, g))
+        r = [res[half, c, :, :, :, group(g)].reshape(CH, GW) for half in range(2)]
 
         def half_of(h):
-            r0 = res[0, c].reshape(CH, HD)
-            r1 = res[1, c].reshape(CH, HD)
             return jnp.concatenate(
-                [dot_nt(r0, w[h, pl.ds(n, 256), pl.ds(0, HD)]) + dot_nt(r1, w[h, pl.ds(n, 256), pl.ds(HD, HD)])
+                [dot_nt(r[0], w[h, pl.ds(n, 256), pl.ds(g * GW, GW)])
+                 + dot_nt(r[1], w[h, pl.ds(n, 256), pl.ds(HD + g * GW, GW)])
                  for n in range(0, HF, 256)], axis=1)
 
-        layer_sum_start(c, 1, half_of)
+        if g == 0:
+            xacc[...] = half_of(1 - core)
+            pown[c] = half_of(core)
+        elif g < NG - 1:
+            xacc[...] += half_of(1 - core)
+            pown[c] += half_of(core)
+        else:
+            xs[1, c] = (xacc[...] + half_of(1 - core)).astype(BF16)
+            share_x(c, 1)
+            pown[c] += half_of(core)
 
     def st_src_t(c):
         src_t[:, pl.ds(c * CH, CH)] = srcb[c].reshape(CH, KP).T
@@ -365,18 +388,17 @@
         outs.append(pltpu.make_async_copy(src, dst, lsem.at[8 + len(outs)]))
         outs[-1].start()
 
-    def st_dec_grad(h):
-        for m in range(0, HF, 256):
-            lhs = feat_t[h, pl.ds(m, 256), :]
-            for half in range(2):
-                for off, n in TILES:
-                    rhs = res[half, :, :, :, :, pl.ds(off, n)].reshape(2 * CH, n)
-                    stag[pl.ds(h * HF + m, 256), pl.ds(half * HD + off, n)] = dot(lhs, rhs).astype(BF16)
-            rows = pl.ds(h * HF + m, 256)
-            put(stag.at[rows], dg_ref.at[0, rows])
+    def st_dec_grad(quarter):
+        rows = pl.ds(quarter * 256, 256)
+        lhs = feat_t[quarter // 2, pl.ds(quarter % 2 * 256, 256), :]
+        for half in range(2):
+            for off, n in TILES:
+                rhs = res[half, :, :, :, :, pl.ds(off, n)].reshape(2 * CH, n)
+                stag[rows, pl.ds(half * HD + off, n)] = dot(lhs, rhs).astype(BF16)
+        put(stag.at[rows], dg_ref.at[0, rows])
 
     def line(c, ph):
-        return [(st_line, c, ph, b) for b in range(4)]
+        return [(st_line, c, ph, b) for b in range(NB)]
 
     def near(c, ph, *bs):
         return [(st_near, c, ph, b) for b in bs]
@@ -385,23 +407,31 @@
         return [(st_far, c, ph, b) for b in bs]
 
     def end(c, ph):
-        return [(st_far_end, c, ph, b) for b in range(4)]
-
-    order = [
-        (st_preact, 0), *line(0, 0), (st_preact, 1), *line(1, 0),
-        *near(0, 0, 0, 1, 2), *far(0, 0, 0), *near(0, 0, 3), *far(0, 0, 1), *near(1, 0, 0), *far(0, 0, 2),
-        *near(1, 0, 1), *far(0, 0, 3), *near(1, 0, 2, 3), *end(0, 0),
-        (st_rebuilt, 0), *far(1, 0, 0, 1, 2, 3), *end(1, 0), (st_ring, 0), (st_transpose, 0), (st_src_t, 0), (st_src_t, 1),
-        (st_second, 0), (st_rebuilt, 1), (st_swap, 0), (st_transpose, 1), (st_ring, 1), (st_swap_pass, 0), (st_second, 1),
-        (st_residual, 0), (st_swap, 1), (st_gather, 0), (st_swap_pass, 1), (st_forward, 0), (st_residual, 1),
-        (st_summed, 0), *line(0, 1), (st_gather, 1),
-        *near(0, 1, 0, 1), (st_forward, 1), *near(0, 1, 2), *far(0, 1, 0), *near(0, 1, 3), *far(0, 1, 1, 2, 3),
-        (st_summed, 1), *line(1, 1), *end(0, 1), (st_dec_grad, 0),
-        *near(1, 1, 0, 1, 2), *far(1, 1, 0), *near(1, 1, 3), *far(1, 1, 1, 2, 3),
-        (st_dec_grad, 1), (st_enc_grad, 0), *end(1, 1), (st_enc_grad, 1),
-    ]
+        return [(st_far_end, c, ph, b) for b in range(NB)]
+
+    timed = []
+    for k, begin in ((0, 16.5), (1, 22.2)):
+        timed += [(15.0 + 2.0 * k, (st_preact, k))]
+        timed += [(16.5 + 1.3 * k + 0.01 * b, line(k, 0)[b]) for b in range(NB)]
+        timed += [(begin + 2.2 + 0.72 * b, near(k, 0, b)[0]) for b in range(NB)]
+        timed += [(begin + 5.4 + 0.72 * b, far(k, 0, b)[0]) for b in range(NB)]
+        timed += [(begin + 8.7 + 0.72 * b, end(k, 0)[b]) for b in range(NB)]
+    steps = ((st_rebuilt, 0), (st_ring, 3.5), (st_second, 7.4), (st_swap, 11.2), (st_residual, 16.7),
+             (st_gather, 20.5), (st_forward, 24.0), (st_summed, 27.8))
+    for c, begin in ((0, 30.5), (1, 38.6)):
+        for stage, lag in steps:
+            timed += [(begin + lag + (1.25 if lag else 0.85) * g, (stage, c, g)) for g in range(NG)]
+        ready = begin + 27.8 + 1.25 * NG
+        timed += [(ready + 0.3 + 0.01 * b, line(c, 1)[b]) for b in range(NB)]
+        timed += [(ready + 3.6 + 0.72 * b, near(c, 1, b)[0]) for b in range(NB)]
+        timed += [(ready + 6.8 + 0.72 * b, far(c, 1, b)[0]) for b in range(NB)]
+        timed += [(ready + 12.6 + 0.01 * b, end(c, 1)[b]) for b in range(NB)]
+        timed += [(ready + 18, (st_enc_grad, c))]
+        timed += [(begin + 5, (st_transpose, c)), (begin + 6, (st_src_t, c))]
+    timed += [(ready + t, (st_dec_grad, i)) for i, t in enumerate((0.6, 2.1, 12.4, 12.41))]
+    order = [entry for _, entry in sorted(timed, key=lambda item: item[0])]
     for stage, *args in order:
-        now[0] = (stage.__name__, *args)
+        now[0] = (stage.__name__, args[0])
         stage(*args)
     put(egout, eg_ref)
     for batch, n in stage_tiles.items():
@@ -416,11 +446,22 @@
     assert len(ids.table) == N_RECV and len(sids.table) == N_SEND, (len(ids.table), len(sids.table))
 
 
+def put_out(eg_in, dg_in, eg_out, dg_out, sem):
+    copies = [pltpu.make_async_copy(eg_in, eg_out, sem.at[0])]
+    for i in range(8):
+        rows = pl.ds(i * 128, 128)
+        copies.append(pltpu.make_async_copy(dg_in.at[0, rows], dg_out.at[0, rows], sem.at[i + 1]))
+    for copy in copies:
+        copy.start()
+    for copy in copies:
+        copy.wait()
+
+
 def step(source, enc_weight, enc_bias, dec_weight, dec_bias, targets):
     vmem = pl.BlockSpec(memory_space=pltpu.VMEM)
     hbm = pl.BlockSpec(memory_space=pltpu.HBM)
     V = pltpu.VMEM
-    return pl.pallas_call(
+    grads = pl.pallas_call(
         kernel,
         out_shape=(
             jax.ShapeDtypeStruct((KD, NF), BF16),
@@ -438,16 +479,17 @@
             V((2, 16, D), BF16),
             V((2, CH, HF), F32),
             V((2, CH, HF), F32),
+            V((CH, HF), F32),
             V((2, 2, CH, HF), BF16),
             V((2, 2, CH, HF), BF16),
             V((2, 2, 2, CH, HF), BF16),
             V((2, 2, CH, HF), BF16),
             V((2, 2, CH, HF), BF16),
             V((2, CH, HF), F32),
-            V((2, 2, 4, 64, HF), BF16),
+            V((2, 2, NB, RB, HF), BF16),
             V((2, HF, 2 * CH), BF16),
             V((KP, 2 * CH), BF16),
-            V((2, 2, 4, 64, HF), BF16),
+            V((2, 2, NB, RB, HF), BF16),
             V((2, KP, HF), F32),
             V((2, 2, 4, 4, 16, HD), BF16),
             V((2, 2, 2, 2, 16, HD), BF16),
@@ -468,6 +510,15 @@
             collective_id=0, has_side_effects=True, vmem_limit_bytes=48 * 1024 * 1024),
     )(*[pltpu.with_memory_space_constraint(a, pltpu.HBM)
         for a in (source, enc_weight, enc_bias.reshape(1, NF), dec_weight, dec_bias, targets)])
+    anywhere = pl.BlockSpec(memory_space=pl.ANY)
+    return pl.pallas_call(
+        put_out,
+        out_shape=tuple(jax.ShapeDtypeStruct(g.shape, g.dtype) for g in grads),
+        in_specs=[anywhere] * 2,
+        out_specs=(anywhere,) * 2,
+        scratch_shapes=[pltpu.SemaphoreType.DMA((9,))],
+        compiler_params=pltpu.CompilerParams(vmem_limit_bytes=1024 * 1024),
+    )(*grads)
 
 
 def solution(mesh):

time: 109 us -> 97.8 us (0.90)
  Pallas kernels: 106 us -> 96.9 us
  local copies, waits for them, and re-layouts: 3 us -> 0 us
    pallas_call x1, Pallas kernels: 106 us -> 94.4 us  [step(): pl.pallas_call(kernel, out_shape=(jax.ShapeDtypeStruct((KD, NF), BF16), j...]
    unnamed x2 -> x0, local copies, waits for them, and re-layouts: 3 us -> none
    pallas_call x0 -> x1, Pallas kernels: none -> 2.45 us  [step(): pl.pallas_call(put_out, out_shape=tuple((jax.ShapeDtypeStruct(g.shape, g....]
where the time goes in v3:
time: 97.8 us; the launch traced here: 97.7 us
  Pallas kernels  96.9 us (99%)
    pallas_call x1, Pallas kernels, step(): pl.pallas_call(kernel, out_shape=(jax.ShapeDtypeStruct((KD, NF), BF16), j...  94.4 us
    pallas_call x1, Pallas kernels, step(): pl.pallas_call(put_out, out_shape=tuple((jax.ShapeDtypeStruct(g.shape, g....  2.45 us

profile of v3, /device:TPU:1, one launch (start us, length us, event | category | flops | bytes accessed | tf_op | source)
XLA Modules:
  0.0 97.7 jit_solution(4615780641313533167)
XLA Ops:
  0.6 94.4 %shard_map.77 = (bf16[288,1024]{1,0:T(8,128)(2,1)S(1)}, bf16[1,1024,2304]{2,1,0:T(8,128)(2,1)S(1)}) custom-call(bf16[16,288]{1,0:T(8,128)(2,1)} %src_hbm.1, bf16[288,1024]{1,0:T(8,128)(2,1)} %encw_ref.1, f32[1,1024]{1,0:T(1,128)} %bitcast.1, bf16[1,1024,2304]{2,1,0:T(8,128)(2,1)} %decw_ref.1, f32[1,2304]{1,0:T(1,128)} %dbias_hbm.1, bf16[1,16,2304]{2,1,0:T(8,128)(2,1)} %tgt_hbm.1), custom_call_target="tpu_custom_call" | custom-call | tf_op jit(solution)/shard_map/pallas_call | solution.py:464
  95.0 2.4 %shard_map.78 = (bf16[288,1024]{1,0:T(8,128)(2,1)}, bf16[1,1024,2304]{2,1,0:T(8,128)(2,1)}) custom-call(bf16[288,1024]{1,0:T(8,128)(2,1)S(1)} %get-tuple-element.4.eg_in, bf16[1,1024,2304]{2,1,0:T(8,128)(2,1)S(1)} %get-tuple-element.5.dg_in), custom_call_target="tpu_custom_call" | custom-call | tf_op jit(solution)/shard_map/pallas_call | solution.py:514

commit v4 on v3

--- a/solution.py
+++ b/solution.py
@@ -18,11 +18,18 @@
 KD = 288
 KP = 384
 CH = 256
-GW = 384
-NG = HD // GW
+GROUPS = ((0, 384), (384, 384), (768, 384))
+NG = len(GROUPS)
 NB = 8
 RB = CH // NB
 TILES = ((0, 256), (256, 256), (512, 256), (768, 256), (1024, 128))
+
+
+OFFSETS = [(dx, dy) for dx in range(4) for dy in range(4) if dx or dy]
+
+
+def hops(offset):
+    return sum(min(d, 4 - d) for d in offset)
 
 
 def dot(a, b):
@@ -93,6 +100,9 @@
             dst = bulk(tiles[name])
         pltpu.make_async_copy(dst, dst, rsem.at[ids[name] + slot]).wait()
 
+    mine_in = lax.rem(zh + x + y, 2)
+    oz = 1 - mine_in
+
     loads = {}
 
     def load(name, src, dst):
@@ -100,7 +110,7 @@
         loads[name].start()
 
     load("src", src_hbm, src_ref)
-    load("tgt", tgt_hbm.at[0], tg.at[zh])
+    load("tgt", tgt_hbm.at[0], tg.at[mine_in])
     load("bias", bias_hbm, bias_ref)
     load("dbias", dbias_hbm, dbias_ref)
     for h in range(2):
@@ -109,7 +119,7 @@
         load(("d", h), decw_ref.at[0, pl.ds(h * HF, HF)], w.at[h])
 
     barrier = pltpu.get_barrier_semaphore()
-    peers = [xy_dev(dx, dy) for dx in range(4) for dy in range(4) if dx or dy]
+    peers = [xy_dev(dx, dy) for dx, dy in OFFSETS]
     peers += [partner_z, partner_c] + [ring_dev(d) for d in (1, -1, 3, -3)]
     for dev in peers:
         pl.semaphore_signal(barrier, inc=1, device_id=dev, device_id_type=MESH)
@@ -117,39 +127,36 @@
     me = x * 4 + y
     zero = jnp.zeros((16, KP - KD), BF16)
     loads['src'].wait()
-    srcb[zh, me] = jnp.concatenate([src_ref[...], zero], axis=1)
+    srcb[mine_in, me] = jnp.concatenate([src_ref[...], zero], axis=1)
     for h in range(2):
         wenc[h, pl.ds(KD, KP - KD)] = jnp.zeros((KP - KD, HF), BF16)
     pl.semaphore_wait(barrier, len(peers))
 
     for i in range(2):
         ids[("src", i)]
-    oz = 1 - zh
-    send(srcb.at[zh, me], srcb.at[zh, me], "srcz", partner_z)
+    send(srcb.at[mine_in, me], srcb.at[mine_in, me], "srcz", partner_z)
 
     def spread(z, batch):
-        for dx in range(4):
-            for dy in range(4):
-                if dx or dy:
-                    send(srcb.at[z, me], srcb.at[z, me], ("src", 0), xy_dev(dx, dy), z, batch=batch)
-
-    @pl.when(zh == 0)
+        for dx, dy in sorted(OFFSETS, key=lambda o: -hops(o)):
+            send(srcb.at[z, me], srcb.at[z, me], ("src", 0), xy_dev(dx, dy), z, batch=batch)
+
+    @pl.when(mine_in == 0)
     def _():
-        spread(zh, "own")
+        spread(mine_in, "own")
 
     recv("srcz")
     now[0] = "relay"
     spread(oz, "relay")
 
-    @pl.when(zh == 1)
+    @pl.when(mine_in == 1)
     def _():
-        spread(zh, "own")
+        spread(mine_in, "own")
 
     tiles[("src", 0)] //= 3
     stage_tiles["own"] //= 2
     for name in ("tgt", "bias", "dbias"):
         loads[name].wait()
-    send(tg.at[zh], tg.at[zh], "tgt", partner_z)
+    send(tg.at[mine_in], tg.at[mine_in], "tgt", partner_z)
 
     is_end = (zl == 0) | (zl == 3)
     is_inner = (zl == 1) | (zl == 2)
@@ -245,8 +252,12 @@
             return ref.at[half, c, a, pl.ds(b, nb), :, cols]
         return ref.at[half, c, pl.ds(b, nb), a, :, cols]
 
+    def tiles_of(g):
+        start, width = GROUPS[g]
+        return [(start + t, min(256, width - t)) for t in range(0, width, 256)]
+
     def group(g):
-        return pl.ds(g * GW, GW)
+        return pl.ds(*GROUPS[g])
 
     def st_rebuilt(c, g):
         if g == 0:
@@ -258,8 +269,7 @@
         f1 = feats[c, 1].reshape(CH, HF)
         cg = group(g)
         for half in range(2):
-            for off, n in ((0, 256), (256, 128)):
-                off = g * GW + off
+            for off, n in tiles_of(g):
                 cols = pl.ds(half * HD + off, n)
                 part = dot(f0, w[0, :, cols]) + dot(f1, w[1, :, cols])
                 rb[half, c, :, :, :, pl.ds(off, n)] = part.astype(BF16).reshape(4, 4, 16, n)
@@ -297,7 +307,7 @@
                      + t2[half, c, 1, :, :, cg].astype(F32))
             qs[half, c, :, :, cg] = total
             us[half, c, :, :, cg] = total.astype(BF16)
-            for j in range(1, 4):
+            for j in (2, 1, 3):
                 send(us.at[half, c, lax.rem(b + j, 4), :, cg], qr.at[half, c, j - 1, :, cg], ("q", c, g), dev(0, j))
 
     def st_swap(c, g):
@@ -318,12 +328,12 @@
         recv(("u", c, g))
         for half in range(2):
             a, b, dev = axes(half)
-            cols = pl.ds(half * HD + g * GW, GW)
+            cols = pl.ds(half * HD + GROUPS[g][0], GROUPS[g][1])
             total = us[half, c, b, :, cg].astype(F32) + ur[half, c, :, cg].astype(F32)
             total = total + dbias_ref[:, cols] - tg[c, :, cols].astype(F32)
             res[half, c, x, y, :, cg] = total.astype(BF16)
             mine = res.at[half, c, x, y, :, cg]
-            for j in range(1, 4):
+            for j in (2, 1, 3):
                 send(mine, mine, ("a", c, g), dev(0, j))
 
     def st_gather(c, g):
@@ -350,12 +360,13 @@
 
     def st_summed(c, g):
         recv(("e", c, g))
-        r = [res[half, c, :, :, :, group(g)].reshape(CH, GW) for half in range(2)]
+        start, width = GROUPS[g]
+        r = [res[half, c, :, :, :, group(g)].reshape(CH, width) for half in range(2)]
 
         def half_of(h):
             return jnp.concatenate(
-                [dot_nt(r[0], w[h, pl.ds(n, 256), pl.ds(g * GW, GW)])
-                 + dot_nt(r[1], w[h, pl.ds(n, 256), pl.ds(HD + g * GW, GW)])
+                [dot_nt(r[0], w[h, pl.ds(n, 256), pl.ds(start, width)])
+                 + dot_nt(r[1], w[h, pl.ds(n, 256), pl.ds(HD + start, width)])
                  for n in range(0, HF, 256)], axis=1)
 
         if g == 0:
@@ -410,15 +421,15 @@
         return [(st_far_end, c, ph, b) for b in range(NB)]
 
     timed = []
-    for k, begin in ((0, 16.5), (1, 22.2)):
-        timed += [(15.0 + 2.0 * k, (st_preact, k))]
-        timed += [(16.5 + 1.3 * k + 0.01 * b, line(k, 0)[b]) for b in range(NB)]
+    for k, begin in ((0, 15.0), (1, 20.7)):
+        timed += [(13.5 + 2.0 * k, (st_preact, k))]
+        timed += [(15.0 + 1.3 * k + 0.01 * b, line(k, 0)[b]) for b in range(NB)]
         timed += [(begin + 2.2 + 0.72 * b, near(k, 0, b)[0]) for b in range(NB)]
         timed += [(begin + 5.4 + 0.72 * b, far(k, 0, b)[0]) for b in range(NB)]
         timed += [(begin + 8.7 + 0.72 * b, end(k, 0)[b]) for b in range(NB)]
     steps = ((st_rebuilt, 0), (st_ring, 3.5), (st_second, 7.4), (st_swap, 11.2), (st_residual, 16.7),
              (st_gather, 20.5), (st_forward, 24.0), (st_summed, 27.8))
-    for c, begin in ((0, 30.5), (1, 38.6)):
+    for c, begin in ((0, 29.0), (1, 35.5)):
         for stage, lag in steps:
             timed += [(begin + lag + (1.25 if lag else 0.85) * g, (stage, c, g)) for g in range(NG)]
         ready = begin + 27.8 + 1.25 * NG

time: 97.8 us -> 97.3 us (level)
  no operation moved by 1% of the time
where the time goes in v4:
time: 97.3 us; the launch traced here: 97.1 us
  Pallas kernels  96.3 us (99%)
    pallas_call x1, Pallas kernels, step(): pl.pallas_call(kernel, out_shape=(jax.ShapeDtypeStruct((KD, NF), BF16), j...  93.9 us
    pallas_call x1, Pallas kernels, step(): pl.pallas_call(put_out, out_shape=tuple((jax.ShapeDtypeStruct(g.shape, g....  2.45 us

profile of v4, /device:TPU:1, one launch (start us, length us, event | category | flops | bytes accessed | tf_op | source)
XLA Modules:
  0.0 97.1 jit_solution(14008051851761987771)
XLA Ops:
  0.6 93.9 %shard_map.77 = (bf16[288,1024]{1,0:T(8,128)(2,1)S(1)}, bf16[1,1024,2304]{2,1,0:T(8,128)(2,1)S(1)}) custom-call(bf16[16,288]{1,0:T(8,128)(2,1)} %src_hbm.1, bf16[288,1024]{1,0:T(8,128)(2,1)} %encw_ref.1, f32[1,1024]{1,0:T(1,128)} %bitcast.1, bf16[1,1024,2304]{2,1,0:T(8,128)(2,1)} %decw_ref.1, f32[1,2304]{1,0:T(1,128)} %dbias_hbm.1, bf16[1,16,2304]{2,1,0:T(8,128)(2,1)} %tgt_hbm.1), custom_call_target="tpu_custom_call" | custom-call | tf_op jit(solution)/shard_map/pallas_call | solution.py:475
  94.5 2.4 %shard_map.78 = (bf16[288,1024]{1,0:T(8,128)(2,1)}, bf16[1,1024,2304]{2,1,0:T(8,128)(2,1)}) custom-call(bf16[288,1024]{1,0:T(8,128)(2,1)S(1)} %get-tuple-element.4.eg_in, bf16[1,1024,2304]{2,1,0:T(8,128)(2,1)S(1)} %get-tuple-element.5.dg_in), custom_call_target="tpu_custom_call" | custom-call | tf_op jit(solution)/shard_map/pallas_call | solution.py:525

commit v5 on v4

--- a/solution.py
+++ b/solution.py
@@ -45,10 +45,12 @@
         self.table = {}
 
     def __getitem__(self, name):
+        if name[0] in ("x", "n", "h"):
+            name = name[:1] + name[2:]
         return self.table.setdefault(name, len(self.table))
 
 
-N_RECV = 122
+N_RECV = 100
 N_SEND = 29
 
 

time: 97.3 us -> 97.1 us (level)
  no operation moved by 1% of the time
where the time goes in v5:
time: 97.1 us; the launch traced here: 96.9 us
  Pallas kernels  96.1 us (99%)
    pallas_call x1, Pallas kernels, step(): pl.pallas_call(kernel, out_shape=(jax.ShapeDtypeStruct((KD, NF), BF16), j...  93.7 us
    pallas_call x1, Pallas kernels, step(): pl.pallas_call(put_out, out_shape=tuple((jax.ShapeDtypeStruct(g.shape, g....  2.45 us

profile of v5, /device:TPU:1, one launch (start us, length us, event | category | flops | bytes accessed | tf_op | source)
XLA Modules:
  0.0 96.9 jit_solution(14540868665764261558)
XLA Ops:
  0.6 93.7 %shard_map.77 = (bf16[288,1024]{1,0:T(8,128)(2,1)S(1)}, bf16[1,1024,2304]{2,1,0:T(8,128)(2,1)S(1)}) custom-call(bf16[16,288]{1,0:T(8,128)(2,1)} %src_hbm.1, bf16[288,1024]{1,0:T(8,128)(2,1)} %encw_ref.1, f32[1,1024]{1,0:T(1,128)} %bitcast.1, bf16[1,1024,2304]{2,1,0:T(8,128)(2,1)} %decw_ref.1, f32[1,2304]{1,0:T(1,128)} %dbias_hbm.1, bf16[1,16,2304]{2,1,0:T(8,128)(2,1)} %tgt_hbm.1), custom_call_target="tpu_custom_call" | custom-call | tf_op jit(solution)/shard_map/pallas_call | solution.py:477
  94.3 2.4 %shard_map.78 = (bf16[288,1024]{1,0:T(8,128)(2,1)}, bf16[1,1024,2304]{2,1,0:T(8,128)(2,1)}) custom-call(bf16[288,1024]{1,0:T(8,128)(2,1)S(1)} %get-tuple-element.4.eg_in, bf16[1,1024,2304]{2,1,0:T(8,128)(2,1)S(1)} %get-tuple-element.5.dg_in), custom_call_target="tpu_custom_call" | custom-call | tf_op jit(solution)/shard_map/pallas_call | solution.py:527
